TPU v7x, 1024 devices: a whole 4x8x16 slice. The times are simulated.
1024 devices in a mesh: ctx: 32 (over x_hi, z), ch: 32 (over x_lo, y, core).
Axes of the slice: x: 4 (x_hi: 2, x_lo: 2; x = x_hi * 2 + x_lo), y: 8, z: 16, core: 2. Of those that a mesh axis runs over, the one named last changes fastest.
Arguments:
- query_proj: bfloat16 [8192, 4096], P('ch', 'ctx'), may hold values from -6 to 6
- key_proj: bfloat16 [8192, 4096], P('ch', 'ctx'), may hold values from -6 to 6
- value_proj: bfloat16 [8192, 4096], P('ch', 'ctx'), may hold values from -6 to 6
- cotangent: bfloat16 [8192, 4096], P('ch', 'ctx'), may hold values from -0.0234375 to 0.0234375
- positions: int32 [4096], P('ctx'), may hold values from 0 to 4095, as said below
- group_of: int32 [8192], replicated, may hold values from 0 to 511, as said below
- decay_rates: float32 [512, 16], replicated, may hold values from 2.4414063e-05 to 0.03
- residues: float32 [512, 16], replicated, may hold values from -1.5 to 1.5
Outputs:
- output: bfloat16 [8192, 4096], P('ch', 'ctx')
- filter_grad: float32 [512, 4096], P('ch', 'ctx')
Inputs may be any that keep to these rules, and one draw needn't show every extreme that they name: positions is a permutation of the sequence positions; every aligned run of 64 stored tokens holds consecutive positions that start at a multiple of 64. `group_of`: every group has exactly 16 channels; each aligned block of 256 channels holds exactly 8 channels of the groups of each aligned block of 16 groups.
All inputs are finite; a program needn't handle non-finite values.
Results may differ from a plain program's by a relative error of at most 0.0058.
Values may be sent and summed in bfloat16 or wider, within the bound.
A program may use at most 32 MiB of HBM per device.

v0:
```python
import math

import jax
import jax.numpy as jnp
from jax import lax
from jax.sharding import PartitionSpec as P


def product(form, left, right):
    return jnp.einsum(form, left, right, precision=lax.Precision.HIGHEST)


def split_rows(extent):
    chosen = 2
    for divisor in range(2, math.isqrt(extent) + 1, 2):
        if extent % divisor == 0:
            chosen = divisor
    return chosen


def dft_tables(row_count, col_count, extent):
    row_index = jnp.arange(row_count, dtype=jnp.int32)
    col_index = jnp.arange(col_count, dtype=jnp.int32)

    def angles(left_index, right_index, modulus):
        phase = left_index[:, None] * right_index[None, :] % modulus
        return phase.astype(jnp.float32) * (2.0 * math.pi / modulus)

    row_angle = angles(row_index, row_index, row_count)
    col_angle = angles(col_index, col_index, col_count)
    twist_angle = angles(row_index, col_index, extent)
    return (
        jnp.cos(row_angle),
        jnp.sin(row_angle),
        jnp.cos(col_angle),
        jnp.sin(col_angle),
        jnp.cos(twist_angle),
        jnp.sin(twist_angle),
    )


def forward_transform(signal, tables, row_count, col_count):
    row_cos, row_sin, col_cos, col_sin, twist_cos, twist_sin = tables
    folded = signal.reshape(signal.shape[0], row_count // 2, col_count)
    mid_real = product("ka,cab->ckb", row_cos[:, : row_count // 2], folded)
    mid_imag = -product("ka,cab->ckb", row_sin[:, : row_count // 2], folded)
    turned_real = mid_real * twist_cos + mid_imag * twist_sin
    turned_imag = mid_imag * twist_cos - mid_real * twist_sin
    spec_real = product("ckb,bm->ckm", turned_real, col_cos) + product(
        "ckb,bm->ckm", turned_imag, col_sin
    )
    spec_imag = product("ckb,bm->ckm", turned_imag, col_cos) - product(
        "ckb,bm->ckm", turned_real, col_sin
    )
    return (spec_real, spec_imag)


def inverse_transform(spec_real, spec_imag, tables, row_count, col_count):
    row_cos, row_sin, col_cos, col_sin, twist_cos, twist_sin = tables
    mid_real = product("ckm,bm->ckb", spec_real, col_cos) - product(
        "ckm,bm->ckb", spec_imag, col_sin
    )
    mid_imag = product("ckm,bm->ckb", spec_imag, col_cos) + product(
        "ckm,bm->ckb", spec_real, col_sin
    )
    turned_real = mid_real * twist_cos - mid_imag * twist_sin
    turned_imag = mid_imag * twist_cos + mid_real * twist_sin
    folded = product("ak,ckb->cab", row_cos[: row_count // 2, :], turned_real) - product(
        "ak,ckb->cab", row_sin[: row_count // 2, :], turned_imag
    )
    return folded.reshape(spec_real.shape[0], -1) / float(row_count * col_count)


def spectra(gated_seq, weighted_seq, chan_groups, decay_rates, residues, seq_length):
    extent = 2 * seq_length
    row_count = split_rows(extent)
    col_count = extent // row_count
    decay_rows = decay_rates[chan_groups]
    gain_rows = residues[chan_groups]
    tap_index = jnp.arange(seq_length, dtype=jnp.float32)
    coefs = gain_rows * jnp.sqrt(2.0 * decay_rows)
    filters = jnp.sum(coefs[:, :, None] * jnp.exp(-decay_rows[:, :, None] * tap_index), axis=1)
    tables = dft_tables(row_count, col_count, extent)
    gated_real, gated_imag = forward_transform(
        gated_seq.astype(jnp.float32), tables, row_count, col_count
    )
    filter_real, filter_imag = forward_transform(filters, tables, row_count, col_count)
    weight_real, weight_imag = forward_transform(
        weighted_seq.astype(jnp.float32), tables, row_count, col_count
    )
    convolved = inverse_transform(
        filter_real * gated_real - filter_imag * gated_imag,
        filter_real * gated_imag + filter_imag * gated_real,
        tables,
        row_count,
        col_count,
    )
    lagged = inverse_transform(
        weight_real * gated_real + weight_imag * gated_imag,
        weight_imag * gated_real - weight_real * gated_imag,
        tables,
        row_count,
        col_count,
    )
    return (convolved, lagged)


def shards(query_proj, key_proj, value_proj, cotangent, positions, group_of, decay_rates, residues):
    ctx_count = lax.axis_size("ctx")
    ctx_rank = lax.axis_index("ctx")
    ch_rank = lax.axis_index("ch")
    local_channels, local_tokens = query_proj.shape
    half_run = local_tokens // 2
    run_count = 2 * ctx_count
    seq_length = local_tokens * ctx_count
    per_device = local_channels // ctx_count
    groups_total = decay_rates.shape[0]
    gated = (key_proj.astype(jnp.float32) * value_proj.astype(jnp.float32)).astype(jnp.bfloat16)
    weighted = (cotangent.astype(jnp.float32) * query_proj.astype(jnp.float32)).astype(jnp.bfloat16)
    run_ids = jnp.stack([positions[0], positions[half_run]]) // half_run
    all_runs = lax.all_gather(run_ids, "ctx", axis=0, tiled=True)
    source_run = (
        jnp.zeros((run_count,), jnp.int32).at[all_runs].set(jnp.arange(run_count, dtype=jnp.int32))
    )

    def to_sequence(stored):
        return stored.reshape(per_device, run_count, half_run)[:, source_run, :].reshape(
            per_device, seq_length
        )

    shard_groups = lax.dynamic_slice_in_dim(group_of, ch_rank * local_channels, local_channels)
    gated_cols, weighted_cols = (
        lax.all_to_all(gated, "ctx", split_axis=0, concat_axis=1, tiled=True),
        lax.all_to_all(weighted, "ctx", split_axis=0, concat_axis=1, tiled=True),
    )
    first_channel = ch_rank * local_channels + ctx_rank * per_device
    chan_groups = lax.dynamic_slice_in_dim(group_of, first_channel, per_device)
    convolved, lagged = spectra(
        to_sequence(gated_cols),
        to_sequence(weighted_cols),
        chan_groups,
        decay_rates,
        residues,
        seq_length,
    )
    ordered = convolved.astype(jnp.bfloat16).reshape(per_device, run_count, half_run)[
        :, all_runs, :
    ]
    conv_tokens = lax.all_to_all(
        ordered.reshape(per_device, seq_length), "ctx", split_axis=1, concat_axis=0, tiled=True
    )
    output = (query_proj.astype(jnp.float32) * conv_tokens.astype(jnp.float32)).astype(jnp.bfloat16)
    lag_rows = lax.all_to_all(lagged, "ctx", split_axis=1, concat_axis=0, tiled=True)
    select_all = (
        jnp.arange(groups_total, dtype=jnp.int32)[:, None] == shard_groups[None, :]
    ).astype(jnp.float32)
    filter_grad = lax.psum_scatter(
        jnp.dot(
            select_all,
            lag_rows,
            precision=lax.Precision.HIGHEST,
            preferred_element_type=jnp.float32,
        ),
        "ch",
        scatter_dimension=0,
        tiled=True,
    )
    return (output, filter_grad)


def solution(mesh):
    placed = (
        P("ch", "ctx"),
        P("ch", "ctx"),
        P("ch", "ctx"),
        P("ch", "ctx"),
        P("ctx"),
        P(),
        P(),
        P(),
    )
    return jax.shard_map(
        shards,
        mesh=mesh,
        in_specs=placed,
        out_specs=(P("ch", "ctx"), P("ch", "ctx")),
        check_vma=False,
    )
```

profile of v0, /device:TPU:1, one launch (start us, length us, event | category | flops | bytes accessed | tf_op | source)
XLA Modules:
  0.0 244.8 jit_solution(11765034710367521252)
XLA Ops:
  7.2 1.5 fusion.40
  8.7 22.3 %all-to-all-start = ((bf16[32,8,128]{2,1,0:T(8,128)(2,1)}), bf16[32,8,128]{2,1,0:T(8,128)(2,1)S(1)}, u32[]{:S(2)}, u32[]{:S(2)}) async-start(bf16[32,8,128]{2,1,0:T(8,128)(2,1)} %fusion.40), calls=%async_computation | async-start | bytes 131072 | tf_op jit(solution)/shard_map/all_to_all | solution.py:133
  31.5 0.8 compare_select_fusion.2
  33.6 0.6 multiply_reduce_fusion
  37.1 0.7 fusion.196
  37.7 1.3 dynamic-slice
  39.6 1.4 fusion.113
  41.1 21.8 %all-reduce = s32[64]{0:T(128)S(1)} all-reduce(s32[64]{0:T(128)S(1)} %fusion.113), channel_id=1, replica_groups=mesh['ctx'=32,'ch'=32] {'ctx'}, use_global_device_ids=true, to_apply=%add | all-reduce | flops 64 | bytes 512
  62.8 0.8 scatter_custom_fusion
  63.7 0.6 fusion.41
  64.3 0.8 dynamic_slice.7
  65.7 7.7 %all-to-all-start.2 = ((bf16[32,8,128]{2,1,0:T(8,128)(2,1)}), bf16[32,8,128]{2,1,0:T(8,128)(2,1)S(1)}, u32[]{:S(2)}, u32[]{:S(2)}) async-start(bf16[32,8,128]{2,1,0:T(8,128)(2,1)} %fusion.41), calls=%async_computation.2 | async-start | bytes 131072 | tf_op jit(solution)/shard_map/all_to_all | solution.py:134
  73.6 0.6 gather_fusion.2
  75.0 12.9 %all-to-all-done.2 = bf16[32,8,128]{2,1,0:T(8,128)(2,1)S(1)} async-done(((bf16[32,8,128]{2,1,0:T(8,128)(2,1)}), bf16[32,8,128]{2,1,0:T(8,128)(2,1)S(1)}, u32[]{:S(2)}, u32[]{:S(2)}) %all-to-all-start.2) | async-done | bytes 65568 | tf_op jit(solution)/shard_map/all_to_all | solution.py:134
  88.1 0.6 gather_fusion.4
  93.9 0.7 multiply_add_fusion
  97.7 0.7 copy.93
  98.4 3.8 %all-to-all-start.3 = ((f32[8,32,128]{2,0,1:T(8,128)}), f32[8,32,128]{2,0,1:T(8,128)S(1)}, u32[]{:S(2)}, u32[]{:S(2)}) async-start(f32[8,32,128]{2,0,1:T(8,128)} %copy.93), calls=%async_computation.3 | async-start | bytes 262144 | tf_op jit(solution)/shard_map/all_to_all | solution.py:153
  105.3 12.8 %all-to-all-done.3 = f32[8,32,128]{2,0,1:T(8,128)S(1)} async-done(((f32[8,32,128]{2,0,1:T(8,128)}), f32[8,32,128]{2,0,1:T(8,128)S(1)}, u32[]{:S(2)}, u32[]{:S(2)}) %all-to-all-start.3) | async-done | bytes 131104 | tf_op jit(solution)/shard_map/all_to_all | solution.py:153
  118.2 1.1 fusion.8
  119.8 0.6 gather_fusion.3
  120.6 17.7 %all_to_all.61 = bf16[8,32,128]{2,0,1:T(8,128)(2,1)S(1)} all-to-all(bf16[8,32,128]{2,0,1:T(8,128)(2,1)S(1)} %copy.87), channel_id=1, replica_groups=mesh['ctx'=32,'ch'=32] {'ctx'}, dimensions={1} | all-to-all | bytes 131072 | tf_op jit(solution)/shard_map/all_to_all | solution.py:149
  138.3 0.6 fusion.24
  138.9 99.0 %reduce-scatter.2.cloned.1.call-done = f32[16,128]{1,0:T(8,128)} async-done(((f32[512,128]{1,0:T(8,128)}), f32[16,128]{1,0:T(8,128)}) %reduce-scatter.2.cloned.1.call-update) | async-done | bytes 8208 | tf_op jit(solution)/shard_map/reduce_scatter | solution.py:157
  (72 shorter events, 18.2 us)
Async XLA Ops:
  7.2 25.1 %copy-start.2 = (f32[512,16]{0,1:T(8,128)S(1)}, f32[512,16]{0,1:T(8,128)}, u32[]{:S(2)}) copy-start(f32[512,16]{0,1:T(8,128)} %param.15) | copy-start | bytes 98308
  8.7 23.7 %copy-start.3 = (f32[512,16]{0,1:T(8,128)S(1)}, f32[512,16]{0,1:T(8,128)}, u32[]{:S(2)}) copy-start(f32[512,16]{0,1:T(8,128)} %param.14) | copy-start | bytes 98308
  8.7 57.0 %all-to-all-start = ((bf16[32,8,128]{2,1,0:T(8,128)(2,1)}), bf16[32,8,128]{2,1,0:T(8,128)(2,1)S(1)}, u32[]{:S(2)}, u32[]{:S(2)}) async-start(bf16[32,8,128]{2,1,0:T(8,128)(2,1)} %fusion.40), calls=%async_computation | async-start | bytes 131072 | tf_op jit(solution)/shard_map/all_to_all | solution.py:133
  36.4 0.7 copy-start.4
  36.4 27.3 %copy-start = (bf16[256,128]{1,0:T(8,128)(2,1)S(1)}, bf16[256,128]{1,0:T(8,128)(2,1)}, u32[]{:S(2)}) copy-start(bf16[256,128]{1,0:T(8,128)(2,1)} %param.8) | copy-start | bytes 196612
  36.4 27.3 %copy-start.1 = (bf16[256,128]{1,0:T(8,128)(2,1)S(1)}, bf16[256,128]{1,0:T(8,128)(2,1)}, u32[]{:S(2)}) copy-start(bf16[256,128]{1,0:T(8,128)(2,1)} %param.11) | copy-start | bytes 196612
  65.7 22.2 %all-to-all-start.2 = ((bf16[32,8,128]{2,1,0:T(8,128)(2,1)}), bf16[32,8,128]{2,1,0:T(8,128)(2,1)S(1)}, u32[]{:S(2)}, u32[]{:S(2)}) async-start(bf16[32,8,128]{2,1,0:T(8,128)(2,1)} %fusion.41), calls=%async_computation.2 | async-start | bytes 131072 | tf_op jit(solution)/shard_map/all_to_all | solution.py:134
  98.4 19.8 %all-to-all-start.3 = ((f32[8,32,128]{2,0,1:T(8,128)}), f32[8,32,128]{2,0,1:T(8,128)S(1)}, u32[]{:S(2)}, u32[]{:S(2)}) async-start(f32[8,32,128]{2,0,1:T(8,128)} %copy.93), calls=%async_computation.3 | async-start | bytes 262144 | tf_op jit(solution)/shard_map/all_to_all | solution.py:153
  102.3 135.7 %reduce-scatter.2.cloned.1.call-start = ((), (), s32[]{:S(2)}) async-start(), calls=%async_computation.5 | async-start | bytes 270336 | tf_op jit(solution)/shard_map/reduce_scatter | solution.py:157
Sparse Core Ops, SparseCore 0:
  119.4 118.5 reduce-scatter.1
where the time goes:
time: 245 us
  waiting for transfers between devices  125 us (51%)
  blocking collectives  39.4 us (16%)
  starting transfers between devices  34.1 us (14%)
  matrix products  16.7 us (7%)
  between operations  15.2 us (6%)
  local copies, waits for them, and re-layouts  8.48 us (3%)
  other arithmetic  6.1 us (2%)
    reduce_scatter x1, waiting for transfers between devices, shards(): lax.psum_scatter(jnp.dot(select_all, lag_rows, precision=lax.Precision.HI...  99 us
    all_to_all x1, starting transfers between devices, shards(): lax.all_to_all(gated, 'ctx', split_axis=0, concat_axis=1, tiled=True)  22.3 us
    unnamed x1, blocking collectives  21.8 us
    all_to_all x1, blocking collectives, shards(): lax.all_to_all(ordered.reshape(per_device, seq_length), 'ctx', split_axis...  17.7 us
    dot_general x30, matrix products, product(): return jnp.einsum(form, left, right, precision=lax.Precision.HIGHEST)  15.7 us
    all_to_all x1, waiting for transfers between devices, shards(): lax.all_to_all(weighted, 'ctx', split_axis=0, concat_axis=1, tiled=True)  12.9 us
    all_to_all x1, waiting for transfers between devices, shards(): lax.all_to_all(lagged, 'ctx', split_axis=1, concat_axis=0, tiled=True)  12.8 us
    all_to_all x1, starting transfers between devices, shards(): lax.all_to_all(weighted, 'ctx', split_axis=0, concat_axis=1, tiled=True)  7.66 us
  transfers between devices with their start and end apart: 4, of which 3 were waited for; matrix products, arithmetic and copies ran while one was open for 7% of the time, Pallas kernels for 0%

commit v1 on v0

v1 whole, which is shorter than its diff:
```python
import functools
import math

import jax
import jax.numpy as jnp
import ml_dtypes
import numpy as np
from jax import lax
from jax.experimental import pallas as pl
from jax.experimental.pallas import tpu as pltpu
from jax.sharding import PartitionSpec as P

MESH = pl.DeviceIdType.MESH
BF16 = jnp.bfloat16
F32 = jnp.float32


def halves(table):
    high = table.astype(ml_dtypes.bfloat16)
    low = (table - high.astype(np.float64)).astype(ml_dtypes.bfloat16)
    return high, low


def make_tables(n, lanes):
    run = lanes // 2
    extent = 2 * lanes * n
    turn = 2.0 * math.pi
    k = np.arange(n)
    j = np.arange(lanes) % run
    m = np.arange(lanes) % run
    par = np.arange(lanes) // run

    def second(angle, mask):
        cos, sin = np.cos(angle) * mask, np.sin(angle) * mask
        return np.block([[cos, -sin], [sin, cos]])

    perm_angle = turn * (j[:, None] * m[None, :] % run) / run
    nat_angle = turn * (np.arange(lanes)[:, None] * (2 * m + par)[None, :] % lanes) / lanes
    seconds = [second(perm_angle, (par == p)[None, :].astype(np.float64)) for p in range(2)]
    seconds.append(second(nat_angle, 1.0))
    second_tab = np.stack([part for table in seconds for part in halves(table)])

    twists = []
    for rows, cols in ((k, j), (k + 2 * n, j), (k, np.arange(lanes))):
        angle = turn * ((2 * rows[:, None] + 1) * cols[None, :] % (2 * extent)) / (2 * extent)
        twists += [np.cos(angle), -np.sin(angle)]
    twist_tab = np.stack(twists).astype(np.float32)

    kk = np.concatenate([k, k, k + 2 * n, k + 2 * n])
    part = np.concatenate([np.zeros(n), np.ones(n)] * 2)
    angle = turn * ((2 * kk[None, :] + 1) * np.arange(2 * n)[:, None] % (8 * n)) / (8 * n)
    first = np.where(part[None, :] == 0, np.cos(angle), -np.sin(angle))
    run_tab = np.concatenate(halves(first), axis=0)

    kn = np.concatenate([k, k])
    partn = np.concatenate([np.zeros(n), np.ones(n)])
    angle = turn * ((2 * kn[:, None] + 1) * k[None, :] % (4 * n)) / (4 * n)
    chunk = np.where(partn[:, None] == 0, np.cos(angle), -np.sin(angle))
    high, low = halves(chunk)
    chunk_fwd = np.concatenate([high, low, high], axis=1)
    scale = 2.0 / extent
    high, low = halves(chunk.T * scale)
    chunk_inv = np.concatenate([high, low, high], axis=1)
    return second_tab, twist_tab, run_tab, np.ascontiguousarray(run_tab.T), chunk_fwd, chunk_inv


def dot(left, right):
    return lax.dot_general(left, right, (((1,), (0,)), ((), ())), preferred_element_type=F32)


def dot_nt(left, right):
    return lax.dot_general(left, right, (((1,), (1,)), ((), ())), preferred_element_type=F32)


def split(value):
    high = value.astype(BF16)
    return high, (value - high.astype(F32)).astype(BF16)


def iota(shape, axis):
    return lax.broadcasted_iota(jnp.int32, shape, axis)


def kernel(
    n,
    slots,
    own,
    order,
    q_hbm, k_hbm, v_hbm, c_hbm, pos_hbm, grp_hbm, dec_hbm, res_hbm,
    sec_hbm, twi_hbm, run_hbm, runt_hbm, cfw_hbm, cin_hbm,
    out_ref, fg_ref,
    q_ref, k_ref, v_ref, c_ref, pos_ref, grp_ref, dec_ref, res_ref,
    sec_ref, twi_ref, run_ref, runt_ref, cfw_ref, cin_ref,
    x_send, x_recv, p_recv, c_send, c_recv, l_send, l_recv, f_send, f_recv,
    xs, taps, gcol, ys, onehot, unsort, lagsel,
    in_sem, x_ssem, x_rsem, p_ssem, p_rsem, c_ssem, c_rsem, l_ssem, l_rsem, f_sem,
):
    lanes = 128
    run = lanes // 2
    chans = n * slots
    ctx = lax.axis_index("ctx")
    ch = lax.axis_index("ch")

    barrier = pltpu.get_barrier_semaphore()

    def greet(step, carry):
        pl.semaphore_signal(
            barrier, inc=1, device_id={"ctx": lax.rem(ctx + step, n)}, device_id_type=MESH
        )
        pl.semaphore_signal(
            barrier, inc=1, device_id={"ch": lax.rem(ch + step, n)}, device_id_type=MESH
        )
        return carry

    lax.fori_loop(1, n, greet, 0)

    sources = (grp_hbm, k_hbm, v_hbm, c_hbm, q_hbm, pos_hbm, dec_hbm, res_hbm,
               runt_hbm, run_hbm, cfw_hbm, twi_hbm, sec_hbm, cin_hbm)
    targets = (grp_ref, k_ref, v_ref, c_ref, q_ref, pos_ref, dec_ref, res_ref,
               runt_ref, run_ref, cfw_ref, twi_ref, sec_ref, cin_ref)
    loads = [
        pltpu.make_async_copy(source, target, in_sem.at[index])
        for index, (source, target) in enumerate(zip(sources, targets))
    ]
    for load in loads:
        load.start()

    loads[0].wait()
    if chans > lanes:
        per_row = chans // lanes
        pieces = [grp_ref[pl.ds(i, n, stride=per_row), :] for i in range(per_row)]
        group_all = jnp.concatenate(pieces, axis=1).astype(F32)
        pieces = [grp_ref[pl.ds(ch * per_row + i, 1), :] for i in range(per_row)]
        group_row = jnp.concatenate(pieces, axis=1).astype(F32)
    else:
        group_all = grp_ref[...].astype(F32)
        group_row = grp_ref[pl.ds(ch, 1), :].astype(F32)
    owner_row = jnp.floor(group_row * (1.0 / own))
    owner_rows = jnp.broadcast_to(owner_row, (chans, chans))
    owner_cols = jnp.transpose(owner_rows)
    row_i = iota((chans, chans), 0)
    col_i = iota((chans, chans), 1)
    same = owner_rows == owner_cols
    rank_row = jnp.sum(jnp.where(same & (row_i < col_i), 1.0, 0.0), axis=0, keepdims=True)
    rank_col = jnp.sum(jnp.where(same & (col_i < row_i), 1.0, 0.0), axis=1, keepdims=True)
    slot_row = owner_row * slots + rank_row
    slot_col = owner_cols[:, 0:1] * slots + rank_col
    sort = jnp.where(slot_row == row_i.astype(F32), 1.0, 0.0).astype(BF16)
    unsort[...] = jnp.where(slot_col == col_i.astype(F32), 1.0, 0.0).astype(BF16)

    for index in range(1, 5):
        loads[index].wait()
    gated = (k_ref[...].astype(F32) * v_ref[...].astype(F32)).astype(BF16)
    weighted = (c_ref[...].astype(F32) * q_ref[...].astype(F32)).astype(BF16)
    gated = dot(sort, gated).reshape(n, slots, lanes)
    weighted = dot(sort, weighted).reshape(n, slots, lanes)
    x_send[...] = jnp.concatenate([gated, weighted], axis=1).astype(BF16)
    loads[5].wait()

    pl.semaphore_wait(barrier, 2 * (n - 1))

    def pos_copy(step, target, home):
        return pltpu.make_async_remote_copy(
            src_ref=pos_ref, dst_ref=p_recv.at[home],
            send_sem=p_ssem.at[step], recv_sem=p_rsem.at[home],
            device_id={"ctx": target}, device_id_type=MESH,
        )

    def x_copy(step, target, home):
        return pltpu.make_async_remote_copy(
            src_ref=x_send.at[target], dst_ref=x_recv.at[home],
            send_sem=x_ssem.at[step], recv_sem=x_rsem.at[home],
            device_id={"ctx": target}, device_id_type=MESH,
        )

    def c_copy(step, target, home):
        return pltpu.make_async_remote_copy(
            src_ref=c_send.at[target], dst_ref=c_recv.at[home],
            send_sem=c_ssem.at[step], recv_sem=c_rsem.at[home],
            device_id={"ctx": target}, device_id_type=MESH,
        )

    def l_copy(step, target, home):
        return pltpu.make_async_remote_copy(
            src_ref=l_send.at[target], dst_ref=l_recv.at[home],
            send_sem=l_ssem.at[step], recv_sem=l_rsem.at[home],
            device_id={"ch": target}, device_id_type=MESH,
        )

    def send_all(copy, me):
        def body(step, carry):
            copy(step, lax.rem(me + step, n), me).start()
            return carry
        lax.fori_loop(1, n, body, 0)

    def recv_all(copy, me):
        def body(step, carry):
            other = lax.rem(me + step, n)
            copy(step, other, other).wait_recv()
            return carry
        lax.fori_loop(1, n, body, 0)

    def sent_all(copy, me):
        def body(step, carry):
            copy(step, lax.rem(me + step, n), me).wait_send()
            return carry
        lax.fori_loop(1, n, body, 0)

    send_all(x_copy, ctx)
    send_all(pos_copy, ctx)
    x_recv[ctx] = x_send[ctx]
    p_recv[ctx] = pos_ref[...]

    loads[6].wait()
    loads[7].wait()
    me_slot = iota((slots, chans), 0).astype(F32) + (ctx * slots).astype(F32)
    mine = jnp.where(slot_row == me_slot, group_row, 0.0)
    my_group = jnp.sum(mine, axis=1, keepdims=True)
    groups_total = dec_ref.shape[1]
    pick = my_group == iota((slots, groups_total), 1).astype(F32)
    rates, coefs = [], []
    for mode in range(order):
        rate = jnp.sum(jnp.where(pick, dec_ref[mode : mode + 1, :], 0.0), axis=1, keepdims=True)
        gain = jnp.sum(jnp.where(pick, res_ref[mode : mode + 1, :], 0.0), axis=1, keepdims=True)
        rates.append(jnp.broadcast_to(-rate, (slots, lanes)))
        coefs.append(jnp.broadcast_to(gain * jnp.sqrt(2.0 * rate), (slots, lanes)))
    lane_time = iota((slots, lanes), 1).astype(F32)

    def tap_step(chunk, carry):
        time = lane_time + (chunk * lanes).astype(F32)
        total = coefs[0] * jnp.exp(rates[0] * time)
        for mode in range(1, order):
            total = total + coefs[mode] * jnp.exp(rates[mode] * time)
        taps[pl.ds(pl.multiple_of(chunk * slots, slots), slots), :] = total
        return carry

    lax.fori_loop(0, n, tap_step, 0)

    for index in range(8, 14):
        loads[index].wait()

    def turned(real, imag, which):
        cos, sin = twi_ref[2 * which], twi_ref[2 * which + 1]
        return real * cos - imag * sin, real * sin + imag * cos

    def turned_back(real, imag, which):
        cos, sin = twi_ref[2 * which], twi_ref[2 * which + 1]
        return real * cos + imag * sin, imag * cos - real * sin

    def second(high, low, which):
        return (
            dot(high, sec_ref[2 * which])
            + dot(low, sec_ref[2 * which])
            + dot(high, sec_ref[2 * which + 1])
        )

    def second_back(high, low, which):
        return (
            dot_nt(high, sec_ref[2 * which])
            + dot_nt(low, sec_ref[2 * which])
            + dot_nt(high, sec_ref[2 * which + 1])
        )

    rows = []
    for i in range(slots):
        high, low = split(taps[pl.ds(i, n, stride=slots), :])
        mid = dot(cfw_ref[...], jnp.concatenate([high, high, low], axis=0))
        rows.append(jnp.concatenate(turned(mid[:n], mid[n:], 2), axis=1))
    high, low = split(jnp.concatenate(rows, axis=0))
    spec = second(high, low, 2)
    filt_re, filt_im = spec[:, :lanes], spec[:, lanes:]

    mine_all = jnp.floor(group_all * (1.0 / own)) == ctx.astype(F32)
    member = jnp.where(mine_all, 1.0, 0.0)
    before = jnp.where(row_i < col_i, 1.0, 0.0).astype(BF16)
    rank_all = dot(member.astype(BF16), before)
    for i in range(slots):
        hit = jnp.where(mine_all & (rank_all == float(i)), group_all, 0.0)
        gcol[pl.ds(i, n, stride=slots), :] = jnp.broadcast_to(
            jnp.sum(hit, axis=1, keepdims=True), (n, lanes)
        )
    first_own = (ctx * own).astype(F32)
    of_group = jnp.where(
        gcol[...] - first_own == iota((chans, lanes), 1).astype(F32), 1.0, 0.0
    )
    lagsel[...] = jnp.transpose(of_group)[: lagsel.shape[0], :].astype(BF16)

    recv_all(pos_copy, ctx)
    places = p_recv[...].reshape(n, lanes).astype(F32) * (1.0 / run)
    place = jnp.concatenate([places[:, 0:1], places[:, run : run + 1]], axis=0)
    place = jnp.concatenate([place, place + float(2 * n)], axis=0)
    onehot[...] = jnp.where(place == iota((4 * n, 4 * n), 1).astype(F32), 1.0, 0.0).astype(BF16)
    first = dot_nt(runt_ref[...], onehot[...]).astype(BF16)
    last = (dot(onehot[...], run_ref[...]) * (2.0 / (2 * lanes * n))).astype(BF16)
    last = jnp.concatenate([last[: 2 * n], last[2 * n :], last[: 2 * n]], axis=1)
    lane_i = iota((n, lanes), 1)
    left = lane_i < run

    recv_all(x_copy, ctx)
    xs[...] = x_recv[...].astype(F32).reshape(2 * chans, lanes)
    gated_rows, weighted_rows = [[], []], [[], []]
    for i in range(slots):
        pair = []
        for row in (i, i + slots):
            value = xs[pl.ds(row, n, stride=2 * slots), :]
            both = jnp.concatenate(
                [jnp.where(left, value, 0.0), jnp.where(left, 0.0, value)], axis=0
            ).astype(BF16)
            pair.append(jnp.concatenate([both, both], axis=0))
        mid = dot(first, jnp.concatenate(pair, axis=1))
        for par in range(2):
            low_row = 2 * n * par
            for rows, off in ((gated_rows, 0), (weighted_rows, lanes)):
                piece = mid[low_row : low_row + 2 * n, off : off + lanes]
                rows[par].append(jnp.concatenate(turned(piece[:n], piece[n:], par), axis=1))

    def spectrum(rows):
        total = None
        for par in range(2):
            high, low = split(jnp.concatenate(rows[par], axis=0))
            term = second(high, low, par)
            total = term if total is None else total + term
        return total[:, :lanes], total[:, lanes:]

    gat_re, gat_im = spectrum(gated_rows)
    wei_re, wei_im = spectrum(weighted_rows)

    def channel(value, i):
        return value[i * n : (i + 1) * n]

    high, low = split(
        jnp.concatenate(
            [wei_re * gat_re + wei_im * gat_im, wei_im * gat_re - wei_re * gat_im], axis=1
        )
    )
    mid = second_back(high, low, 2)
    for i in range(slots):
        piece = channel(mid, i)
        high, low = split(
            jnp.concatenate(turned_back(piece[:, :lanes], piece[:, lanes:], 2), axis=0)
        )
        ys[pl.ds(i, n, stride=slots), :] = dot(
            cin_ref[...], jnp.concatenate([high, high, low], axis=0)
        )
    l_send[...] = ys[...].reshape(n, slots, lanes).astype(BF16)
    send_all(l_copy, ch)
    l_recv[ch] = l_send[ch]

    high, low = split(
        jnp.concatenate(
            [filt_re * gat_re - filt_im * gat_im, filt_re * gat_im + filt_im * gat_re], axis=1
        )
    )
    mids = [second_back(high, low, par) for par in range(2)]
    for i in range(slots):
        stack = []
        for par in range(2):
            piece = channel(mids[par], i)
            stack += list(turned_back(piece[:, :lanes], piece[:, lanes:], par))
        high, low = split(jnp.concatenate(stack, axis=0))
        value = dot(last, jnp.concatenate([high, high, low], axis=0))
        ys[pl.ds(i, n, stride=slots), :] = jnp.where(left, value[:n], value[n:])
    c_send[...] = ys[...].reshape(n, slots, lanes).astype(BF16)
    send_all(c_copy, ctx)
    c_recv[ctx] = c_send[ctx]

    recv_all(l_copy, ch)
    sums = dot(lagsel[...], l_recv[...].astype(F32).reshape(chans, lanes).astype(BF16))
    f_send[...] = sums[: f_send.shape[0]]
    far = pltpu.make_async_remote_copy(
        src_ref=f_send, dst_ref=f_recv, send_sem=f_sem.at[0], recv_sem=f_sem.at[1],
        device_id={"ctx": ch, "ch": ctx}, device_id_type=MESH,
    )

    @pl.when(ctx != ch)
    def _():
        far.start()

    recv_all(c_copy, ctx)
    conv = dot(unsort[...], c_recv[...].astype(F32).reshape(chans, lanes).astype(BF16))
    out_ref[...] = (q_ref[...].astype(F32) * conv).astype(BF16)

    sent_all(pos_copy, ctx)
    sent_all(x_copy, ctx)
    sent_all(l_copy, ch)
    sent_all(c_copy, ctx)

    @pl.when(ctx != ch)
    def _():
        far.wait()
        fg_ref[...] = f_recv[...]

    @pl.when(ctx == ch)
    def _():
        fg_ref[...] = f_send[...]


def shards(query_proj, key_proj, value_proj, cotangent, positions, group_of, decay_rates, residues):
    n = lax.axis_size("ctx")
    chans, lanes = query_proj.shape
    slots = chans // n
    groups_total, order = decay_rates.shape
    own = groups_total // lax.axis_size("ch")
    own_pad = -(-own // 16) * 16
    width = min(chans, lanes)
    tables = make_tables(n, lanes)
    args = (
        query_proj, key_proj, value_proj, cotangent,
        positions.reshape(1, lanes), group_of.reshape(-1, width),
        decay_rates.T, residues.T,
    ) + tuple(jnp.asarray(table) for table in tables)
    any_spec = pl.BlockSpec(memory_space=pl.ANY)
    vmem_spec = pl.BlockSpec(memory_space=pltpu.VMEM)
    dma = pltpu.SemaphoreType.DMA
    return pl.pallas_call(
        functools.partial(kernel, n, slots, own, order),
        out_shape=(
            jax.ShapeDtypeStruct((chans, lanes), BF16),
            jax.ShapeDtypeStruct((own, lanes), F32),
        ),
        in_specs=[any_spec] * len(args),
        out_specs=(vmem_spec, vmem_spec),
        scratch_shapes=[pltpu.VMEM(arg.shape, arg.dtype) for arg in args]
        + [
            pltpu.VMEM((n, 2 * slots, lanes), BF16),
            pltpu.VMEM((n, 2 * slots, lanes), BF16),
            pltpu.VMEM((n, 1, lanes), jnp.int32),
            pltpu.VMEM((n, slots, lanes), BF16),
            pltpu.VMEM((n, slots, lanes), BF16),
            pltpu.VMEM((n, slots, lanes), BF16),
            pltpu.VMEM((n, slots, lanes), BF16),
            pltpu.VMEM((own, lanes), F32),
            pltpu.VMEM((own, lanes), F32),
            pltpu.VMEM((2 * chans, lanes), F32),
            pltpu.VMEM((chans, lanes), F32),
            pltpu.VMEM((chans, lanes), F32),
            pltpu.VMEM((chans, lanes), F32),
            pltpu.VMEM((4 * n, 4 * n), BF16),
            pltpu.VMEM((chans, chans), BF16),
            pltpu.VMEM((own_pad, chans), BF16),
            dma((len(args),)),
            dma((n,)), dma((n,)), dma((n,)), dma((n,)),
            dma((n,)), dma((n,)), dma((n,)), dma((n,)),
            dma((2,)),
        ],
        compiler_params=pltpu.CompilerParams(collective_id=0, has_side_effects=True),
    )(*args)


def solution(mesh):
    placed = (
        P("ch", "ctx"),
        P("ch", "ctx"),
        P("ch", "ctx"),
        P("ch", "ctx"),
        P("ctx"),
        P(),
        P(),
        P(),
    )
    return jax.shard_map(
        shards,
        mesh=mesh,
        in_specs=placed,
        out_specs=(P("ch", "ctx"), P("ch", "ctx")),
        check_vma=False,
    )
```

time: 245 us -> 57.1 us (0.23)
  the two profiles are of different devices: /device:TPU:1 before, /device:TPU:35 now
where the time goes in v1:
time: 57.1 us; the launch traced here: 56.9 us
  Pallas kernels  54.2 us (95%)
  local copies, waits for them, and re-layouts  2.08 us (4%)
  between operations  0.65 us (1%)
    pallas_call x1, Pallas kernels, shards(): pl.pallas_call(functools.partial(kernel, n, slots, own, order), out_shape...  54.2 us
    unnamed x4, local copies, waits for them, and re-layouts  2.08 us

profile of v1, /device:TPU:35, one launch (start us, length us, event | category | flops | bytes accessed | tf_op | source)
XLA Modules:
  0.0 56.9 jit_solution(8796671100638877908)
XLA Ops:
  0.6 54.2 %shard_map.149 = (bf16[256,128]{1,0:T(8,128)(2,1)}, f32[16,128]{1,0:T(8,128)}) custom-call(bf16[256,128]{1,0:T(8,128)(2,1)} %q_hbm.1, bf16[256,128]{1,0:T(8,128)(2,1)} %k_hbm.1, bf16[256,128]{1,0:T(8,128)(2,1)} %v_hbm.1, bf16[256,128]{1,0:T(8,128)(2,1)} %c_hbm.1, s32[1,128]{1,0:T(1,128)} %bitcast.7, s32[64,128]{1,0:T(8,128)} %bitcast.4, f32[16,512]{1,0:T(8,128)} %bitcast.5, ...), custom_call_target="tpu_custom_call" | custom-call | tf_op jit(solution)/shard_map/pallas_call | solution.py:415
  54.8 0.0 copy-start
  54.8 1.5 %copy.18 = bf16[256,128]{1,0:T(8,128)(2,1)} copy(bf16[256,128]{1,0:T(8,128)(2,1)} %get-tuple-element.4) | data formatting | bytes 131072
  56.3 0.0 copy-done
  56.3 0.6 %copy.19 = f32[16,128]{1,0:T(8,128)} copy(f32[16,128]{1,0:T(8,128)S(1)} %copy-done) | data formatting | bytes 16384
Async XLA Ops:
  54.8 1.5 %copy-start = (f32[16,128]{1,0:T(8,128)S(1)}, f32[16,128]{1,0:T(8,128)}, u32[]{:S(2)}) copy-start(f32[16,128]{1,0:T(8,128)} %get-tuple-element.5) | copy-start | bytes 24580

commit v2 on v1

--- a/solution.py
+++ b/solution.py
@@ -75,6 +75,18 @@
 def split(value):
     high = value.astype(BF16)
     return high, (value - high.astype(F32)).astype(BF16)
+
+
+def partners(n, unit):
+    ring = n // 2
+    steps = [(half, low) for half in range(2) for low in range(ring) if half or low]
+    return sorted(steps, key=lambda s: -(min(s[1], ring - s[1]) / unit + (3 - unit) * s[0]))
+
+
+def moved(index, step, n):
+    ring = n // 2
+    half = lax.rem(index // ring + step[0], 2)
+    return half * ring + lax.rem(lax.rem(index, ring) + step[1], ring)
 
 
 def iota(shape, axis):
@@ -101,19 +113,6 @@
     ctx = lax.axis_index("ctx")
     ch = lax.axis_index("ch")
 
-    barrier = pltpu.get_barrier_semaphore()
-
-    def greet(step, carry):
-        pl.semaphore_signal(
-            barrier, inc=1, device_id={"ctx": lax.rem(ctx + step, n)}, device_id_type=MESH
-        )
-        pl.semaphore_signal(
-            barrier, inc=1, device_id={"ch": lax.rem(ch + step, n)}, device_id_type=MESH
-        )
-        return carry
-
-    lax.fori_loop(1, n, greet, 0)
-
     sources = (grp_hbm, k_hbm, v_hbm, c_hbm, q_hbm, pos_hbm, dec_hbm, res_hbm,
                runt_hbm, run_hbm, cfw_hbm, twi_hbm, sec_hbm, cin_hbm)
     targets = (grp_ref, k_ref, v_ref, c_ref, q_ref, pos_ref, dec_ref, res_ref,
@@ -122,8 +121,21 @@
         pltpu.make_async_copy(source, target, in_sem.at[index])
         for index, (source, target) in enumerate(zip(sources, targets))
     ]
-    for load in loads:
+    for load in loads[:5]:
         load.start()
+    ctx_steps = partners(n, 1)
+    ch_steps = partners(n, 2)
+    barrier = pltpu.get_barrier_semaphore()
+    for step in ctx_steps:
+        pl.semaphore_signal(
+            barrier, inc=1, device_id={"ctx": moved(ctx, step, n)}, device_id_type=MESH
+        )
+    for load in loads[5:]:
+        load.start()
+    for step in ch_steps:
+        pl.semaphore_signal(
+            barrier, inc=1, device_id={"ch": moved(ch, step, n)}, device_id_type=MESH
+        )
 
     loads[0].wait()
     if chans > lanes:
@@ -159,55 +171,43 @@
 
     pl.semaphore_wait(barrier, 2 * (n - 1))
 
-    def pos_copy(step, target, home):
+    def pos_copy(target):
         return pltpu.make_async_remote_copy(
-            src_ref=pos_ref, dst_ref=p_recv.at[home],
-            send_sem=p_ssem.at[step], recv_sem=p_rsem.at[home],
+            src_ref=pos_ref, dst_ref=p_recv.at[ctx], send_sem=p_ssem, recv_sem=p_rsem,
             device_id={"ctx": target}, device_id_type=MESH,
         )
 
-    def x_copy(step, target, home):
+    def x_copy(target):
         return pltpu.make_async_remote_copy(
-            src_ref=x_send.at[target], dst_ref=x_recv.at[home],
-            send_sem=x_ssem.at[step], recv_sem=x_rsem.at[home],
+            src_ref=x_send.at[target], dst_ref=x_recv.at[ctx], send_sem=x_ssem, recv_sem=x_rsem,
             device_id={"ctx": target}, device_id_type=MESH,
         )
 
-    def c_copy(step, target, home):
+    def c_copy(target):
         return pltpu.make_async_remote_copy(
-            src_ref=c_send.at[target], dst_ref=c_recv.at[home],
-            send_sem=c_ssem.at[step], recv_sem=c_rsem.at[home],
+            src_ref=c_send.at[target], dst_ref=c_recv.at[ctx], send_sem=c_ssem, recv_sem=c_rsem,
             device_id={"ctx": target}, device_id_type=MESH,
         )
 
-    def l_copy(step, target, home):
+    flip = (1, n // 4)
+
+    def l_copy(target):
         return pltpu.make_async_remote_copy(
-            src_ref=l_send.at[target], dst_ref=l_recv.at[home],
-            send_sem=l_ssem.at[step], recv_sem=l_rsem.at[home],
+            src_ref=l_send.at[moved(target, flip, n)], dst_ref=l_recv.at[ch],
+            send_sem=l_ssem, recv_sem=l_rsem,
             device_id={"ch": target}, device_id_type=MESH,
         )
 
-    def send_all(copy, me):
-        def body(step, carry):
-            copy(step, lax.rem(me + step, n), me).start()
-            return carry
-        lax.fori_loop(1, n, body, 0)
-
-    def recv_all(copy, me):
-        def body(step, carry):
-            other = lax.rem(me + step, n)
-            copy(step, other, other).wait_recv()
-            return carry
-        lax.fori_loop(1, n, body, 0)
-
-    def sent_all(copy, me):
-        def body(step, carry):
-            copy(step, lax.rem(me + step, n), me).wait_send()
-            return carry
-        lax.fori_loop(1, n, body, 0)
-
-    send_all(x_copy, ctx)
-    send_all(pos_copy, ctx)
+    def send_all(copy, me, steps):
+        for step in steps:
+            copy(moved(me, step, n)).start()
+
+    def await_all(ref, sem):
+        part = ref.at[pl.ds(0, n - 1)]
+        pltpu.make_async_copy(part, part, sem).wait()
+
+    send_all(pos_copy, ctx, ctx_steps)
+    send_all(x_copy, ctx, ctx_steps)
     x_recv[ctx] = x_send[ctx]
     p_recv[ctx] = pos_ref[...]
 
@@ -285,7 +285,7 @@
     )
     lagsel[...] = jnp.transpose(of_group)[: lagsel.shape[0], :].astype(BF16)
 
-    recv_all(pos_copy, ctx)
+    await_all(p_recv, p_rsem)
     places = p_recv[...].reshape(n, lanes).astype(F32) * (1.0 / run)
     place = jnp.concatenate([places[:, 0:1], places[:, run : run + 1]], axis=0)
     place = jnp.concatenate([place, place + float(2 * n)], axis=0)
@@ -296,7 +296,7 @@
     lane_i = iota((n, lanes), 1)
     left = lane_i < run
 
-    recv_all(x_copy, ctx)
+    await_all(x_recv, x_rsem)
     xs[...] = x_recv[...].astype(F32).reshape(2 * chans, lanes)
     gated_rows, weighted_rows = [[], []], [[], []]
     for i in range(slots):
@@ -343,8 +343,8 @@
             cin_ref[...], jnp.concatenate([high, high, low], axis=0)
         )
     l_send[...] = ys[...].reshape(n, slots, lanes).astype(BF16)
-    send_all(l_copy, ch)
-    l_recv[ch] = l_send[ch]
+    send_all(l_copy, ch, ch_steps)
+    l_recv[ch] = l_send[moved(ch, flip, n)]
 
     high, low = split(
         jnp.concatenate(
@@ -361,38 +361,28 @@
         value = dot(last, jnp.concatenate([high, high, low], axis=0))
         ys[pl.ds(i, n, stride=slots), :] = jnp.where(left, value[:n], value[n:])
     c_send[...] = ys[...].reshape(n, slots, lanes).astype(BF16)
-    send_all(c_copy, ctx)
+    send_all(c_copy, ctx, ctx_steps)
     c_recv[ctx] = c_send[ctx]
 
-    recv_all(l_copy, ch)
+    await_all(p_recv, p_ssem)
+    await_all(x_send, x_ssem)
+    await_all(l_recv, l_rsem)
     sums = dot(lagsel[...], l_recv[...].astype(F32).reshape(chans, lanes).astype(BF16))
     f_send[...] = sums[: f_send.shape[0]]
     far = pltpu.make_async_remote_copy(
         src_ref=f_send, dst_ref=f_recv, send_sem=f_sem.at[0], recv_sem=f_sem.at[1],
-        device_id={"ctx": ch, "ch": ctx}, device_id_type=MESH,
-    )
-
-    @pl.when(ctx != ch)
-    def _():
-        far.start()
-
-    recv_all(c_copy, ctx)
+        device_id={"ctx": moved(ch, flip, n), "ch": ctx}, device_id_type=MESH,
+    )
+    far.start()
+
+    await_all(l_send, l_ssem)
+    await_all(c_recv, c_rsem)
     conv = dot(unsort[...], c_recv[...].astype(F32).reshape(chans, lanes).astype(BF16))
     out_ref[...] = (q_ref[...].astype(F32) * conv).astype(BF16)
 
-    sent_all(pos_copy, ctx)
-    sent_all(x_copy, ctx)
-    sent_all(l_copy, ch)
-    sent_all(c_copy, ctx)
-
-    @pl.when(ctx != ch)
-    def _():
-        far.wait()
-        fg_ref[...] = f_recv[...]
-
-    @pl.when(ctx == ch)
-    def _():
-        fg_ref[...] = f_send[...]
+    await_all(c_send, c_ssem)
+    far.wait()
+    fg_ref[...] = f_recv[...]
 
 
 def shards(query_proj, key_proj, value_proj, cotangent, positions, group_of, decay_rates, residues):
@@ -415,8 +405,8 @@
     return pl.pallas_call(
         functools.partial(kernel, n, slots, own, order),
         out_shape=(
-            jax.ShapeDtypeStruct((chans, lanes), BF16),
-            jax.ShapeDtypeStruct((own, lanes), F32),
+            pltpu.VMEM((chans, lanes), BF16),
+            pltpu.VMEM((own, lanes), F32),
         ),
         in_specs=[any_spec] * len(args),
         out_specs=(vmem_spec, vmem_spec),
@@ -439,8 +429,8 @@
             pltpu.VMEM((chans, chans), BF16),
             pltpu.VMEM((own_pad, chans), BF16),
             dma((len(args),)),
-            dma((n,)), dma((n,)), dma((n,)), dma((n,)),
-            dma((n,)), dma((n,)), dma((n,)), dma((n,)),
+            dma(()), dma(()), dma(()), dma(()),
+            dma(()), dma(()), dma(()), dma(()),
             dma((2,)),
         ],
         compiler_params=pltpu.CompilerParams(collective_id=0, has_side_effects=True),

time: 57.1 us -> 48.8 us (0.85)
  the two profiles are of different devices: /device:TPU:35 before, /device:TPU:1 now
where the time goes in v2:
time: 48.8 us; the launch traced here: 48.7 us
  Pallas kernels  46.8 us (96%)
  local copies, waits for them, and re-layouts  1.23 us (3%)
  between operations  0.64 us (1%)
    pallas_call x1, Pallas kernels, shards(): pl.pallas_call(functools.partial(kernel, n, slots, own, order), out_shape...  46.8 us
    unnamed x2, local copies, waits for them, and re-layouts  1.23 us

profile of v2, /device:TPU:1, one launch (start us, length us, event | category | flops | bytes accessed | tf_op | source)
XLA Modules:
  0.0 48.7 jit_solution(13403933872399331768)
XLA Ops:
  0.6 46.8 %shard_map.149 = (bf16[256,128]{1,0:T(8,128)(2,1)S(1)}, f32[16,128]{1,0:T(8,128)S(1)}) custom-call(bf16[256,128]{1,0:T(8,128)(2,1)} %q_hbm.1, bf16[256,128]{1,0:T(8,128)(2,1)} %k_hbm.1, bf16[256,128]{1,0:T(8,128)(2,1)} %v_hbm.1, bf16[256,128]{1,0:T(8,128)(2,1)} %c_hbm.1, s32[1,128]{1,0:T(1,128)} %bitcast.7, s32[64,128]{1,0:T(8,128)} %bitcast.4, ...), custom_call_target="tpu_custom_call" | custom-call | tf_op jit(solution)/shard_map/pallas_call | solution.py:405
  47.4 0.6 %copy.18 = bf16[256,128]{1,0:T(8,128)(2,1)} copy(bf16[256,128]{1,0:T(8,128)(2,1)S(1)} %get-tuple-element.2) | data formatting | bytes 131072
  48.1 0.6 %copy.19 = f32[16,128]{1,0:T(8,128)} copy(f32[16,128]{1,0:T(8,128)S(1)} %get-tuple-element.3) | data formatting | bytes 16384

commit v3 on v2

--- a/solution.py
+++ b/solution.py
@@ -85,8 +85,7 @@
 
 def moved(index, step, n):
     ring = n // 2
-    half = lax.rem(index // ring + step[0], 2)
-    return half * ring + lax.rem(lax.rem(index, ring) + step[1], ring)
+    return ((index + step[0] * ring) & ring) + ((index + step[1]) & (ring - 1))
 
 
 def iota(shape, axis):
@@ -121,8 +120,6 @@
         pltpu.make_async_copy(source, target, in_sem.at[index])
         for index, (source, target) in enumerate(zip(sources, targets))
     ]
-    for load in loads[:5]:
-        load.start()
     ctx_steps = partners(n, 1)
     ch_steps = partners(n, 2)
     barrier = pltpu.get_barrier_semaphore()
@@ -130,7 +127,7 @@
         pl.semaphore_signal(
             barrier, inc=1, device_id={"ctx": moved(ctx, step, n)}, device_id_type=MESH
         )
-    for load in loads[5:]:
+    for load in loads:
         load.start()
     for step in ch_steps:
         pl.semaphore_signal(
@@ -385,6 +382,17 @@
     fg_ref[...] = f_recv[...]
 
 
+def put_kernel(out_ref, fg_ref, out_hbm, fg_hbm, sem):
+    puts = [
+        pltpu.make_async_copy(out_ref, out_hbm, sem.at[0]),
+        pltpu.make_async_copy(fg_ref, fg_hbm, sem.at[1]),
+    ]
+    for put in puts:
+        put.start()
+    for put in puts:
+        put.wait()
+
+
 def shards(query_proj, key_proj, value_proj, cotangent, positions, group_of, decay_rates, residues):
     n = lax.axis_size("ctx")
     chans, lanes = query_proj.shape
@@ -402,7 +410,7 @@
     any_spec = pl.BlockSpec(memory_space=pl.ANY)
     vmem_spec = pl.BlockSpec(memory_space=pltpu.VMEM)
     dma = pltpu.SemaphoreType.DMA
-    return pl.pallas_call(
+    output, filter_grad = pl.pallas_call(
         functools.partial(kernel, n, slots, own, order),
         out_shape=(
             pltpu.VMEM((chans, lanes), BF16),
@@ -435,6 +443,19 @@
         ],
         compiler_params=pltpu.CompilerParams(collective_id=0, has_side_effects=True),
     )(*args)
+    return pl.pallas_call(
+        put_kernel,
+        out_shape=(
+            jax.ShapeDtypeStruct((chans, lanes), BF16),
+            jax.ShapeDtypeStruct((own, lanes), F32),
+        ),
+        in_specs=[vmem_spec, vmem_spec],
+        out_specs=(any_spec, any_spec),
+        scratch_shapes=[dma((2,))],
+    )(
+        pltpu.with_memory_space_constraint(output, pltpu.VMEM),
+        pltpu.with_memory_space_constraint(filter_grad, pltpu.VMEM),
+    )
 
 
 def solution(mesh):

time: 48.8 us -> 48.3 us (0.990)
  local copies, waits for them, and re-layouts: 1.23 us -> 0 us
  Pallas kernels: 46.8 us -> 47.5 us
    unnamed x2 -> x0, local copies, waits for them, and re-layouts: 1.23 us -> none
    pallas_call x0 -> x1, Pallas kernels: none -> 0.65 us  [shards(): pl.pallas_call(put_kernel, out_shape=(jax.ShapeDtypeStruct((chans, lanes)...]
where the time goes in v3:
time: 48.3 us; the launch traced here: 48.1 us
  Pallas kernels  47.5 us (98%)
  between operations  0.64 us (1%)
    pallas_call x1, Pallas kernels, shards(): pl.pallas_call(functools.partial(kernel, n, slots, own, order), out_shape...  46.8 us

profile of v3, /device:TPU:1, one launch (start us, length us, event | category | flops | bytes accessed | tf_op | source)
XLA Modules:
  0.0 48.1 jit_solution(16814326645039294304)
XLA Ops:
  0.6 46.8 %shard_map.149 = (bf16[256,128]{1,0:T(8,128)(2,1)S(1)}, f32[16,128]{1,0:T(8,128)S(1)}) custom-call(bf16[256,128]{1,0:T(8,128)(2,1)} %q_hbm.1, bf16[256,128]{1,0:T(8,128)(2,1)} %k_hbm.1, bf16[256,128]{1,0:T(8,128)(2,1)} %v_hbm.1, bf16[256,128]{1,0:T(8,128)(2,1)} %c_hbm.1, s32[1,128]{1,0:T(1,128)} %bitcast.7, s32[64,128]{1,0:T(8,128)} %bitcast.4, ...), custom_call_target="tpu_custom_call" | custom-call | tf_op jit(solution)/shard_map/pallas_call | solution.py:413
  47.4 0.7 %shard_map.150 = (bf16[256,128]{1,0:T(8,128)(2,1)}, f32[16,128]{1,0:T(8,128)}) custom-call(bf16[256,128]{1,0:T(8,128)(2,1)S(1)} %get-tuple-element.4.out_ref, f32[16,128]{1,0:T(8,128)S(1)} %get-tuple-element.5.fg_ref), custom_call_target="tpu_custom_call" | custom-call | tf_op jit(solution)/shard_map/pallas_call | solution.py:446

commit v4 on v3

--- a/solution.py
+++ b/solution.py
@@ -27,18 +27,20 @@
     turn = 2.0 * math.pi
     k = np.arange(n)
     j = np.arange(lanes) % run
-    m = np.arange(lanes) % run
-    par = np.arange(lanes) // run
-
-    def second(angle, mask):
-        cos, sin = np.cos(angle) * mask, np.sin(angle) * mask
+    m = np.arange(run)
+
+    def second(angle):
+        cos, sin = np.cos(angle), np.sin(angle)
         return np.block([[cos, -sin], [sin, cos]])
 
-    perm_angle = turn * (j[:, None] * m[None, :] % run) / run
-    nat_angle = turn * (np.arange(lanes)[:, None] * (2 * m + par)[None, :] % lanes) / lanes
-    seconds = [second(perm_angle, (par == p)[None, :].astype(np.float64)) for p in range(2)]
-    seconds.append(second(nat_angle, 1.0))
-    second_tab = np.stack([part for table in seconds for part in halves(table)])
+    perm = second(turn * (j[:, None] * m[None, :] % run) / run)
+    lane = np.arange(lanes)
+    nat = [
+        second(turn * (lane[:, None] * (2 * m + p)[None, :] % lanes) / lanes) for p in range(2)
+    ]
+    second_tab = np.stack(
+        [np.concatenate(halves(perm), axis=1), *halves(np.concatenate(nat, axis=1))]
+    )
 
     twists = []
     for rows, cols in ((k, j), (k + 2 * n, j), (k, np.arange(lanes))):
@@ -114,7 +116,7 @@
 
     sources = (grp_hbm, k_hbm, v_hbm, c_hbm, q_hbm, pos_hbm, dec_hbm, res_hbm,
                runt_hbm, run_hbm, cfw_hbm, twi_hbm, sec_hbm, cin_hbm)
-    targets = (grp_ref, k_ref, v_ref, c_ref, q_ref, pos_ref, dec_ref, res_ref,
+    targets = (grp_ref.at[pl.ds(0, grp_hbm.shape[0])], k_ref, v_ref, c_ref, q_ref, pos_ref, dec_ref, res_ref,
                runt_ref, run_ref, cfw_ref, twi_ref, sec_ref, cin_ref)
     loads = [
         pltpu.make_async_copy(source, target, in_sem.at[index])
@@ -142,7 +144,7 @@
         pieces = [grp_ref[pl.ds(ch * per_row + i, 1), :] for i in range(per_row)]
         group_row = jnp.concatenate(pieces, axis=1).astype(F32)
     else:
-        group_all = grp_ref[...].astype(F32)
+        group_all = grp_ref[:n, :].astype(F32)
         group_row = grp_ref[pl.ds(ch, 1), :].astype(F32)
     owner_row = jnp.floor(group_row * (1.0 / own))
     owner_rows = jnp.broadcast_to(owner_row, (chans, chans))
@@ -203,8 +205,9 @@
         part = ref.at[pl.ds(0, n - 1)]
         pltpu.make_async_copy(part, part, sem).wait()
 
-    send_all(pos_copy, ctx, ctx_steps)
-    send_all(x_copy, ctx, ctx_steps)
+    for step in ctx_steps:
+        pos_copy(moved(ctx, step, n)).start()
+        x_copy(moved(ctx, step, n)).start()
     x_recv[ctx] = x_send[ctx]
     p_recv[ctx] = pos_ref[...]
 
@@ -244,19 +247,10 @@
         cos, sin = twi_ref[2 * which], twi_ref[2 * which + 1]
         return real * cos + imag * sin, imag * cos - real * sin
 
-    def second(high, low, which):
-        return (
-            dot(high, sec_ref[2 * which])
-            + dot(low, sec_ref[2 * which])
-            + dot(high, sec_ref[2 * which + 1])
-        )
-
-    def second_back(high, low, which):
-        return (
-            dot_nt(high, sec_ref[2 * which])
-            + dot_nt(low, sec_ref[2 * which])
-            + dot_nt(high, sec_ref[2 * which + 1])
-        )
+    half = iota((1, lanes), 1) < run
+
+    def swapped(value):
+        return pltpu.roll(value, run, axis=1)
 
     rows = []
     for i in range(slots):
@@ -264,8 +258,8 @@
         mid = dot(cfw_ref[...], jnp.concatenate([high, high, low], axis=0))
         rows.append(jnp.concatenate(turned(mid[:n], mid[n:], 2), axis=1))
     high, low = split(jnp.concatenate(rows, axis=0))
-    spec = second(high, low, 2)
-    filt_re, filt_im = spec[:, :lanes], spec[:, lanes:]
+    spec = dot(high, sec_ref[1]) + dot(low, sec_ref[1]) + dot(high, sec_ref[2])
+    filt = jnp.concatenate([spec[:, :lanes], spec[:, lanes:]], axis=0)
 
     mine_all = jnp.floor(group_all * (1.0 / own)) == ctx.astype(F32)
     member = jnp.where(mine_all, 1.0, 0.0)
@@ -278,7 +272,7 @@
         )
     first_own = (ctx * own).astype(F32)
     of_group = jnp.where(
-        gcol[...] - first_own == iota((chans, lanes), 1).astype(F32), 1.0, 0.0
+        gcol[:chans, :] - first_own == iota((chans, lanes), 1).astype(F32), 1.0, 0.0
     )
     lagsel[...] = jnp.transpose(of_group)[: lagsel.shape[0], :].astype(BF16)
 
@@ -294,7 +288,7 @@
     left = lane_i < run
 
     await_all(x_recv, x_rsem)
-    xs[...] = x_recv[...].astype(F32).reshape(2 * chans, lanes)
+    xs[: 2 * chans, :] = x_recv[...].astype(F32).reshape(2 * chans, lanes)
     gated_rows, weighted_rows = [[], []], [[], []]
     for i in range(slots):
         pair = []
@@ -312,25 +306,22 @@
                 rows[par].append(jnp.concatenate(turned(piece[:n], piece[n:], par), axis=1))
 
     def spectrum(rows):
-        total = None
-        for par in range(2):
-            high, low = split(jnp.concatenate(rows[par], axis=0))
-            term = second(high, low, par)
-            total = term if total is None else total + term
-        return total[:, :lanes], total[:, lanes:]
-
-    gat_re, gat_im = spectrum(gated_rows)
-    wei_re, wei_im = spectrum(weighted_rows)
+        high, low = split(jnp.concatenate(rows[0] + rows[1], axis=0))
+        both = dot(high, sec_ref[0])
+        return both[:, :lanes] + both[:, lanes:] + dot(low, sec_ref[0, :, :lanes])
+
+    gat = spectrum(gated_rows)
+    wei = spectrum(weighted_rows)
+    turned_gat = swapped(gat)
+    gat_re = jnp.where(half, gat, turned_gat)
+    gat_im = jnp.where(half, turned_gat, -gat)
 
     def channel(value, i):
         return value[i * n : (i + 1) * n]
 
-    high, low = split(
-        jnp.concatenate(
-            [wei_re * gat_re + wei_im * gat_im, wei_im * gat_re - wei_re * gat_im], axis=1
-        )
-    )
-    mid = second_back(high, low, 2)
+    product = wei * gat_re + swapped(wei) * gat_im
+    high, low = split(jnp.concatenate([product[:chans], product[chans:]], axis=1))
+    mid = dot_nt(high, sec_ref[1]) + dot_nt(low, sec_ref[1]) + dot_nt(high, sec_ref[2])
     for i in range(slots):
         piece = channel(mid, i)
         high, low = split(
@@ -339,25 +330,23 @@
         ys[pl.ds(i, n, stride=slots), :] = dot(
             cin_ref[...], jnp.concatenate([high, high, low], axis=0)
         )
-    l_send[...] = ys[...].reshape(n, slots, lanes).astype(BF16)
+    l_send[...] = ys[:chans, :].reshape(n, slots, lanes).astype(BF16)
     send_all(l_copy, ch, ch_steps)
     l_recv[ch] = l_send[moved(ch, flip, n)]
 
-    high, low = split(
-        jnp.concatenate(
-            [filt_re * gat_re - filt_im * gat_im, filt_re * gat_im + filt_im * gat_re], axis=1
-        )
-    )
-    mids = [second_back(high, low, par) for par in range(2)]
+    high, low = split(filt * gat_re - swapped(filt) * gat_im)
+    mid = dot_nt(jnp.concatenate([high, high], axis=1), sec_ref[0]) + dot_nt(
+        low, sec_ref[0, :, :lanes]
+    )
     for i in range(slots):
         stack = []
         for par in range(2):
-            piece = channel(mids[par], i)
+            piece = channel(mid, par * slots + i)
             stack += list(turned_back(piece[:, :lanes], piece[:, lanes:], par))
         high, low = split(jnp.concatenate(stack, axis=0))
         value = dot(last, jnp.concatenate([high, high, low], axis=0))
         ys[pl.ds(i, n, stride=slots), :] = jnp.where(left, value[:n], value[n:])
-    c_send[...] = ys[...].reshape(n, slots, lanes).astype(BF16)
+    c_send[...] = ys[:chans, :].reshape(n, slots, lanes).astype(BF16)
     send_all(c_copy, ctx, ctx_steps)
     c_recv[ctx] = c_send[ctx]
 
@@ -418,7 +407,10 @@
         ),
         in_specs=[any_spec] * len(args),
         out_specs=(vmem_spec, vmem_spec),
-        scratch_shapes=[pltpu.VMEM(arg.shape, arg.dtype) for arg in args]
+        scratch_shapes=[
+            pltpu.VMEM((arg.shape[0] + 8 * (at == 5),) + arg.shape[1:], arg.dtype)
+            for at, arg in enumerate(args)
+        ]
         + [
             pltpu.VMEM((n, 2 * slots, lanes), BF16),
             pltpu.VMEM((n, 2 * slots, lanes), BF16),
@@ -429,10 +421,10 @@
             pltpu.VMEM((n, slots, lanes), BF16),
             pltpu.VMEM((own, lanes), F32),
             pltpu.VMEM((own, lanes), F32),
-            pltpu.VMEM((2 * chans, lanes), F32),
-            pltpu.VMEM((chans, lanes), F32),
-            pltpu.VMEM((chans, lanes), F32),
-            pltpu.VMEM((chans, lanes), F32),
+            pltpu.VMEM((2 * chans + 2 * slots, lanes), F32),
+            pltpu.VMEM((chans + slots, lanes), F32),
+            pltpu.VMEM((chans + slots, lanes), F32),
+            pltpu.VMEM((chans + slots, lanes), F32),
             pltpu.VMEM((4 * n, 4 * n), BF16),
             pltpu.VMEM((chans, chans), BF16),
             pltpu.VMEM((own_pad, chans), BF16),

time: 48.3 us -> 48 us (level)
  no operation moved by 1% of the time
where the time goes in v4:
time: 48 us; the launch traced here: 47.9 us
  Pallas kernels  47.2 us (98%)
  between operations  0.64 us (1%)
    pallas_call x1, Pallas kernels, shards(): pl.pallas_call(functools.partial(kernel, n, slots, own, order), out_shape...  46.6 us

profile of v4, /device:TPU:1, one launch (start us, length us, event | category | flops | bytes accessed | tf_op | source)
XLA Modules:
  0.0 47.9 jit_solution(7217331410770010440)
XLA Ops:
  0.6 46.6 %shard_map.149 = (bf16[256,128]{1,0:T(8,128)(2,1)S(1)}, f32[16,128]{1,0:T(8,128)S(1)}) custom-call(bf16[256,128]{1,0:T(8,128)(2,1)} %q_hbm.1, bf16[256,128]{1,0:T(8,128)(2,1)} %k_hbm.1, bf16[256,128]{1,0:T(8,128)(2,1)} %v_hbm.1, bf16[256,128]{1,0:T(8,128)(2,1)} %c_hbm.1, s32[1,128]{1,0:T(1,128)} %bitcast.7, s32[64,128]{1,0:T(8,128)} %bitcast.4, ...), custom_call_target="tpu_custom_call" | custom-call | tf_op jit(solution)/shard_map/pallas_call | solution.py:402
  47.2 0.7 %shard_map.150 = (bf16[256,128]{1,0:T(8,128)(2,1)}, f32[16,128]{1,0:T(8,128)}) custom-call(bf16[256,128]{1,0:T(8,128)(2,1)S(1)} %get-tuple-element.4.out_ref, f32[16,128]{1,0:T(8,128)S(1)} %get-tuple-element.5.fg_ref), custom_call_target="tpu_custom_call" | custom-call | tf_op jit(solution)/shard_map/pallas_call | solution.py:438

commit v5 on v4

--- a/solution.py
+++ b/solution.py
@@ -38,14 +38,23 @@
     nat = [
         second(turn * (lane[:, None] * (2 * m + p)[None, :] % lanes) / lanes) for p in range(2)
     ]
+    by_par = np.zeros((2, 2, run, 2, lanes))
+    for p in range(2):
+        by_par[:, p, :, p, :] = perm.reshape(2, 2, run, lanes)[:, 0]
+    by_par = by_par.reshape(2 * lanes, 2 * lanes)
     second_tab = np.stack(
-        [np.concatenate(halves(perm), axis=1), *halves(np.concatenate(nat, axis=1))]
+        [
+            np.concatenate(halves(perm), axis=1),
+            *halves(np.concatenate(nat, axis=1)),
+            *halves(by_par),
+        ]
     )
 
     twists = []
     for rows, cols in ((k, j), (k + 2 * n, j), (k, np.arange(lanes))):
         angle = turn * ((2 * rows[:, None] + 1) * cols[None, :] % (2 * extent)) / (2 * extent)
         twists += [np.cos(angle), -np.sin(angle)]
+    twists += [np.concatenate([twists[i][:, :run], twists[i + 2][:, :run]], axis=1) for i in (0, 1)]
     twist_tab = np.stack(twists).astype(np.float32)
 
     kk = np.concatenate([k, k, k + 2 * n, k + 2 * n])
@@ -289,7 +298,7 @@
 
     await_all(x_recv, x_rsem)
     xs[: 2 * chans, :] = x_recv[...].astype(F32).reshape(2 * chans, lanes)
-    gated_rows, weighted_rows = [[], []], [[], []]
+    gated_rows, weighted_rows = [], []
     for i in range(slots):
         pair = []
         for row in (i, i + slots):
@@ -299,16 +308,15 @@
             ).astype(BF16)
             pair.append(jnp.concatenate([both, both], axis=0))
         mid = dot(first, jnp.concatenate(pair, axis=1))
-        for par in range(2):
-            low_row = 2 * n * par
-            for rows, off in ((gated_rows, 0), (weighted_rows, lanes)):
-                piece = mid[low_row : low_row + 2 * n, off : off + lanes]
-                rows[par].append(jnp.concatenate(turned(piece[:n], piece[n:], par), axis=1))
+        for rows, off in ((gated_rows, 0), (weighted_rows, lanes)):
+            even, odd = mid[: 2 * n, off : off + lanes], mid[2 * n :, off : off + lanes]
+            piece = jnp.where(half, even, odd) + swapped(jnp.where(half, odd, even))
+            rows.append(jnp.concatenate(turned(piece[:n], piece[n:], 3), axis=1))
 
     def spectrum(rows):
-        high, low = split(jnp.concatenate(rows[0] + rows[1], axis=0))
-        both = dot(high, sec_ref[0])
-        return both[:, :lanes] + both[:, lanes:] + dot(low, sec_ref[0, :, :lanes])
+        high, low = split(jnp.concatenate(rows, axis=0))
+        spec = dot(high, sec_ref[3]) + dot(low, sec_ref[3]) + dot(high, sec_ref[4])
+        return jnp.concatenate([spec[:, :lanes], spec[:, lanes:]], axis=0)
 
     gat = spectrum(gated_rows)
     wei = spectrum(weighted_rows)

time: 48 us -> 48.1 us (level)
  no operation moved by 1% of the time
where the time goes in v5:
time: 48.1 us; the launch traced here: 48 us
  Pallas kernels  47.3 us (98%)
  between operations  0.64 us (1%)
    pallas_call x1, Pallas kernels, shards(): pl.pallas_call(functools.partial(kernel, n, slots, own, order), out_shape...  46.7 us

profile of v5, /device:TPU:1, one launch (start us, length us, event | category | flops | bytes accessed | tf_op | source)
XLA Modules:
  0.0 48.0 jit_solution(14929669489070809720)
XLA Ops:
  0.6 46.7 %shard_map.149 = (bf16[256,128]{1,0:T(8,128)(2,1)S(1)}, f32[16,128]{1,0:T(8,128)S(1)}) custom-call(bf16[256,128]{1,0:T(8,128)(2,1)} %q_hbm.1, bf16[256,128]{1,0:T(8,128)(2,1)} %k_hbm.1, bf16[256,128]{1,0:T(8,128)(2,1)} %v_hbm.1, bf16[256,128]{1,0:T(8,128)(2,1)} %c_hbm.1, s32[1,128]{1,0:T(1,128)} %bitcast.7, s32[64,128]{1,0:T(8,128)} %bitcast.4, ...), custom_call_target="tpu_custom_call" | custom-call | tf_op jit(solution)/shard_map/pallas_call | solution.py:410
  47.3 0.7 %shard_map.150 = (bf16[256,128]{1,0:T(8,128)(2,1)}, f32[16,128]{1,0:T(8,128)}) custom-call(bf16[256,128]{1,0:T(8,128)(2,1)S(1)} %get-tuple-element.4.out_ref, f32[16,128]{1,0:T(8,128)S(1)} %get-tuple-element.5.fg_ref), custom_call_target="tpu_custom_call" | custom-call | tf_op jit(solution)/shard_map/pallas_call | solution.py:446
